TPU v7x, 32 devices: a whole 2x2x4 slice. The times are simulated.
32 devices in a mesh: ctx: 4 (over x, core), tp: 8 (over z, y).
Axes of the slice: x: 2, y: 2, z: 4, core: 2. Of those that a mesh axis runs over, the one named last changes fastest.
Arguments:
- token_ids: int32 [1024], replicated, may hold values from 0 to 128255
- doc_lengths: int32 [8], replicated, may hold values from 1 to 256, 1024 in all
- block_order: int32 [8], replicated, may hold values from 0 to 7, each once
- table: bfloat16 [128256, 8192], P('tp', 'ctx'), may hold values from -6 to 6
- gain: float32 [8192], replicated, may hold values from 0.5 to 12, as said below
- w_query: bfloat16 [8192, 8192], P('ctx', 'tp'), may hold values from -0.0625 to 0.0625
- w_keyval: bfloat16 [8192, 2, 1024], P('ctx'), may hold values from -0.0625 to 0.0625
Outputs:
- attended: bfloat16 [1024, 8192], P('ctx', 'tp')
Inputs may be any that keep to these rules, and one draw needn't show every extreme that they name: `token_ids`: ids of the vocabulary. `doc_lengths`: the documents fill the slab in order, their lengths sum to 1024. `block_order`: a permutation of the 8 blocks of the slab. `gain`: positive gains.
All inputs are finite; a program needn't handle non-finite values.
Results may differ from a plain program's by a relative error of at most 0.007.
The roundings to bfloat16 on the way count: a program that leaves them out, or rounds other values in their place, can miss the bound.
Values may be sent and summed in bfloat16 or wider, within the bound.
A program may use at most 128 MiB of HBM per device.

v0:
```python
import jax
import jax.numpy as jnp
from jax import lax
from jax.sharding import PartitionSpec as P

HEADS = 64
KV_HEADS = 8
HD = 128
BLOCK = 128


rotary_base = 500000.0


def rotary(values_in, pos_rows):
    half_dim = values_in.shape[-1] // 2
    steps_up = jnp.arange(half_dim, dtype=jnp.float32)
    freqs = jnp.power(rotary_base, -2.0 * steps_up / values_in.shape[-1])
    angle = pos_rows.astype(jnp.float32)[:, None] * freqs[None, :]
    angle = angle.reshape((angle.shape[0],) + (1,) * (values_in.ndim - 2) + (half_dim,))
    cosine = jnp.cos(angle)
    sine = jnp.sin(angle)
    first = values_in[..., :half_dim]
    second = values_in[..., half_dim:]
    return jnp.concatenate(
        [first * cosine - second * sine, second * cosine + first * sine], axis=-1
    )


def document_of(pos_rows, doc_lengths):
    ends = jnp.cumsum(doc_lengths)
    return jnp.sum((ends[None, :] <= pos_rows[:, None]).astype(jnp.int32), axis=1)


def shards(token_ids, doc_lengths, block_order, table, gain, w_query, w_keyval):
    ctx_count = lax.axis_size("ctx")
    ctx_at = lax.axis_index("ctx")
    tp_count = lax.axis_size("tp")
    tp_at = lax.axis_index("tp")
    tokens_all = token_ids.shape[0]
    tok_here = tokens_all // ctx_count
    vocab_here = table.shape[0]
    columns = table.shape[1]
    width = gain.shape[0]
    heads_here = HEADS // tp_count
    row_index = jnp.arange(tokens_all, dtype=jnp.int32)
    positions = block_order[row_index // BLOCK] * BLOCK + row_index % BLOCK
    local_ids = token_ids[positions] - tp_at * vocab_here
    inside = (local_ids >= 0) & (local_ids < vocab_here)
    picked = jnp.take(table, jnp.clip(local_ids, 0, vocab_here - 1), axis=0)
    partial_value = jnp.where(inside[:, None], picked, jnp.zeros_like(picked))
    kv_head = tp_at * heads_here // (HEADS // KV_HEADS)
    w_pair = lax.dynamic_slice_in_dim(w_keyval, kv_head * HD, HD, 2).reshape(
        w_keyval.shape[0], 2 * HD
    )
    col_embed = lax.psum(partial_value, "tp").astype(jnp.float32)
    gain_here = lax.dynamic_slice_in_dim(gain, ctx_at * columns, columns)
    col_scaled = (col_embed * gain_here).astype(jnp.bfloat16)
    query_term = jnp.dot(col_scaled, w_query, preferred_element_type=jnp.float32)
    pair_term = jnp.dot(col_scaled, w_pair, preferred_element_type=jnp.float32)
    square_term = jnp.sum(col_embed * col_embed, axis=1)
    query_raw, pair_raw, sumsq = (
        lax.psum_scatter(query_term, "ctx", scatter_dimension=0, tiled=True),
        lax.psum_scatter(pair_term, "ctx", scatter_dimension=0, tiled=True),
        lax.psum_scatter(square_term, "ctx", scatter_dimension=0, tiled=True),
    )
    inverse = lax.rsqrt(sumsq / width + 1e-05)
    my_pos = lax.dynamic_slice_in_dim(positions, ctx_at * tok_here, tok_here)
    query_rows = rotary(
        (query_raw * inverse[:, None]).reshape(tok_here, heads_here, HD), my_pos
    ).astype(jnp.bfloat16)
    key_rows = rotary(pair_raw[:, :HD] * inverse[:, None], my_pos).astype(jnp.bfloat16)
    value_rows = (pair_raw[:, HD:] * inverse[:, None]).astype(jnp.bfloat16)
    my_doc = document_of(my_pos, doc_lengths)
    stacked = jnp.transpose(query_rows, (1, 0, 2)).reshape(heads_here * tok_here, HD)
    query_pos = jnp.tile(my_pos, heads_here)
    query_doc = jnp.tile(my_doc, heads_here)
    inv_root = 1.0 / jnp.sqrt(jnp.float32(HD))
    query_total = heads_here * tok_here
    key_piece = lax.all_gather(key_rows, "ctx", axis=0, tiled=True)
    value_piece = lax.all_gather(value_rows, "ctx", axis=0, tiled=True)
    key_doc = document_of(positions, doc_lengths)
    allowed = (key_doc[None, :] == query_doc[:, None]) & (positions[None, :] <= query_pos[:, None])
    largest = jnp.full((query_total,), -1e30, jnp.float32)
    scores = (
        lax.dot_general(
            stacked, key_piece, (((1,), (1,)), ((), ())), preferred_element_type=jnp.float32
        )
        * inv_root
    )
    masked = jnp.where(allowed, scores, jnp.float32(-1e30))
    new_largest = jnp.maximum(largest, jnp.max(masked, axis=1))
    weights = jnp.where(allowed, jnp.exp(masked - new_largest[:, None]), jnp.float32(0.0))
    new_totals = jnp.sum(weights, axis=1)
    new_accum = jnp.dot(
        weights.astype(jnp.bfloat16), value_piece, preferred_element_type=jnp.float32
    )
    mixed = (new_accum / new_totals[:, None]).reshape(heads_here, tok_here, HD)
    return jnp.transpose(mixed, (1, 0, 2)).reshape(tok_here, heads_here * HD).astype(jnp.bfloat16)


def solution(mesh):
    in_specs = (P(), P(), P(), P("tp", "ctx"), P(), P("ctx", "tp"), P("ctx", None, None))
    out_specs = P("ctx", "tp")
    return jax.shard_map(shards, mesh=mesh, in_specs=in_specs, out_specs=out_specs, check_vma=False)
```

profile of v0, /device:TPU:1, one launch (start us, length us, event | category | flops | bytes accessed | tf_op | source)
XLA Modules:
  0.0 327.2 jit_solution(2111878941764237552)
XLA Ops:
  6.5 0.0 copy-start
  6.5 0.0 all-reduce.3.cloned.1.call-start
  6.6 1.6 fusion.32
  8.2 4.3 %compare_select_fusion.3 = s32[1024,1]{0,1:T(1,128)S(1)} fusion(s32[]{:T(128)} %bitcast.3, s32[]{:T(128)} %bitcast.4, s32[]{:T(128)} %bitcast.5, s32[]{:T(128)} %bitcast.6, s32[]{:T(128)} %bitcast.7, s32[]{:T(128)} %bitcast.9, s32[]{:T(128)} %bitcast.8), kind=kLoop, calls=%fused_computation.38 | loop fusion | flops 23552 | bytes 4124 | tf_op jit(solution)/shard_map/gather | solution.py:47
  12.5 0.7 fusion.21
  13.2 0.0 copy-done
  13.2 4.5 %gather_fusion = s32[1024]{0:T(1024)S(1)} fusion(s32[1024]{0:T(1024)S(1)} %copy-done, s32[1024]{0:T(1024)S(1)} %broadcast_clamp_fusion.1), kind=kCustom, calls=%fused_computation | custom fusion | bytes 12288 | tf_op jit(solution)/shard_map/gather | solution.py:48
  17.8 51.9 %gather_fusion.1 = bf16[1024,2048]{1,0:T(8,128)(2,1)} fusion(bf16[16032,2048]{1,0:T(8,128)(2,1)} %param.10, s32[1024]{0:T(1024)S(1)} %broadcast_clamp_fusion), kind=kCustom, calls=%fused_computation.1 | custom fusion | bytes 8392704 | tf_op jit(solution)/shard_map/jit(_take)/gather | solution.py:50
  69.7 4.1 %select_select_fusion = bf16[1024,2048]{1,0:T(8,128)(2,1)} fusion(bf16[1024,2048]{1,0:T(8,128)(2,1)} %gather_fusion.1, pred[1024]{0:T(1024)(128)(4,1)S(1)} %get-tuple-element.9, pred[1024]{0:T(1024)(128)(4,1)S(1)} %get-tuple-element.19), kind=kLoop, calls=%fused_computation.12 | loop fusion | flops 4194304 | bytes 8390656 | tf_op jit(solution)/shard_map/jit(_where)/select_n | solution.py:51
  73.7 0.0 all-reduce.3.cloned.1.call-update
  73.7 0.0 reduce-scatter.5.cloned.1.call-start
  73.8 0.7 dynamic_slice.10
  74.5 1.8 constant_dynamic-slice_fusion
  76.3 156.2 %all-reduce.3.cloned.1.call-done = bf16[1024,2048]{1,0:T(8,128)(2,1)} async-done(((bf16[1024,2048]{1,0:T(8,128)(2,1)}), bf16[1024,2048]{1,0:T(8,128)(2,1)}) %all-reduce.3.cloned.1.call-update) | async-done | bytes 4194320 | tf_op jit(solution)/shard_map/psum | solution.py:56
  232.5 4.4 %fusion.7 = f32[1024,256]{1,0:T(8,128)} fusion(bf16[1024,2048]{1,0:T(8,128)(2,1)} %all-reduce.3.cloned.1.call-done, f32[2048]{0:T(1024)S(1)} %dynamic_slice.10, bf16[256,8,2,128]{3,2,1,0:T(2,128)(2,1)S(1)} %bitcast.44), kind=kOutput, calls=%fused_computation.14 | convolution fusion | flops 1080033280 | bytes 6299648 | tf_op jit(solution)/shard_map/dot_general | solution.py:60
  236.9 0.0 reduce-scatter.5.cloned.1.call-update
  237.0 0.0 copy-start.2
  237.0 0.0 copy-start.3
  237.0 0.0 reduce-scatter.3.cloned.1.call-start
  237.0 9.9 %fusion.9 = f32[1024,1024]{1,0:T(8,128)} fusion(bf16[2048,1024]{1,0:T(8,128)(2,1)} %param.12, bf16[1024,2048]{1,0:T(8,128)(2,1)} %all-reduce.3.cloned.1.call-done, f32[2048]{0:T(1024)S(1)} %dynamic_slice.10), kind=kOutput, calls=%fused_computation.15 | convolution fusion | flops 4301258752 | bytes 12591104 | tf_op jit(solution)/shard_map/dot_general | solution.py:59
  247.0 0.0 reduce-scatter.3.cloned.1.call-update
  247.0 0.0 copy-done.2
  247.0 0.2 reduce-window.8
  247.2 0.1 fusion.30
  247.3 0.1 convert_reduce_fusion.1
  247.4 0.0 copy-done.3
  247.4 0.6 dynamic-slice
  248.6 0.1 convert_reduce_fusion
  248.7 3.1 fusion.1
  251.8 6.1 %all-reduce = f32[1024]{0:T(1024)S(1)} all-reduce(f32[1024]{0:T(1024)S(1)} %fusion.1), channel_id=3, replica_groups=mesh['ctx'=4,'tp'=8] {'ctx'}, use_global_device_ids=true, to_apply=%region_6.7.clone | all-reduce | flops 1024 | bytes 8192
  257.9 0.1 fusion.26
  258.0 3.0 reduce-scatter.5.cloned.1.call-done
  261.0 1.1 slice_multiply_fusion.1
  262.1 0.6 subtract_convert_fusion.1
  262.7 0.1 pad_maximum_fusion.1
  262.8 6.4 %all_gather.6 = bf16[1024,128]{1,0:T(8,128)(2,1)S(1)} all-gather(bf16[256,128]{1,0:T(8,128)(2,1)S(1)} %pad_maximum_fusion.1), channel_id=1, replica_groups=mesh['ctx'=4,'tp'=8] {'ctx'}, dimensions={0}, use_global_device_ids=true | all-gather | bytes 327680 | tf_op jit(solution)/shard_map/all_gather | solution.py:80
  269.2 6.0 %all_gather.7 = bf16[1024,128]{1,0:T(8,128)(2,1)S(1)} all-gather(bf16[256,128]{1,0:T(8,128)(2,1)S(1)} %get-tuple-element.16), channel_id=1, replica_groups=mesh['ctx'=4,'tp'=8] {'ctx'}, dimensions={0}, use_global_device_ids=true | all-gather | bytes 327680 | tf_op jit(solution)/shard_map/all_gather | solution.py:81
  275.2 32.9 %reduce-scatter.3.cloned.1.call-done = f32[256,1024]{1,0:T(8,128)} async-done(((f32[1024,1024]{1,0:T(8,128)}), f32[256,1024]{1,0:T(8,128)}) %reduce-scatter.3.cloned.1.call-update) | async-done | bytes 1048592 | tf_op jit(solution)/shard_map/reduce_scatter | solution.py:63
  308.1 1.4 multiply_bitcast_fusion
  309.5 0.2 copy.23
  309.7 0.3 fusion.31
  310.0 0.4 subtract_convert_fusion
  310.4 0.3 pad_maximum_fusion
  310.7 2.1 fusion.2
  312.9 0.0 copy-start.1
  312.9 3.8 %fusion.3 = f32[2048]{0:T(1024)S(1)} fusion(f32[2048,1024]{0,1:T(8,128)S(1)} %get-tuple-element.31, f32[2048]{0:T(1024)S(1)} %broadcast_maximum_fusion, s32[2048]{0:T(1024)S(1)} %bitcast.51, s32[2048]{0:T(1024)S(1)} %bitcast.48, s32[1024]{0:T(1024)S(1)} %get-tuple-element.7, s32[1024]{0:T(1024)S(1)} %convert_reduce_fusion), kind=kLoop, calls=%fused_computation.10 | loop fusion | flops 16775168 | bytes 8429568 | tf_op jit(solution)/shard_map/reduce_sum | solution.py:94
  316.7 3.1 fusion.14
  319.8 0.9 copy.34
  320.7 0.0 copy-done.1
  (12 shorter events, 0.1 us)
Async XLA Ops:
  6.5 6.6 %copy-start = (s32[1024]{0:T(1024)S(1)}, s32[1024]{0:T(1024)}, u32[]{:S(2)}) copy-start(s32[1024]{0:T(1024)} %param.7) | copy-start | bytes 12292
  6.5 226.0 %all-reduce.3.cloned.1.call-start = ((), (), s32[]{:S(2)}) async-start(), calls=%async_computation.2 | async-start | bytes 8388608 | tf_op jit(solution)/shard_map/psum | solution.py:56
  73.7 187.3 %reduce-scatter.5.cloned.1.call-start = ((), (), s32[]{:S(2)}) async-start(), calls=%async_computation.4 | async-start | bytes 1310720 | tf_op jit(solution)/shard_map/reduce_scatter | solution.py:64
  237.0 10.0 %copy-start.2 = (s32[8]{0:T(128)S(1)}, s32[8]{0:T(128)}, u32[]{:S(2)}) copy-start(s32[8]{0:T(128)} %param.8) | copy-start | bytes 100
  237.0 10.4 %copy-start.3 = (u32[32]{0:T(128)S(1)}, u32[32]{0:T(128)}, u32[]{:S(2)}) copy-start(u32[32]{0:T(128)} %constant.126) | copy-start | bytes 388
  237.0 71.1 %reduce-scatter.3.cloned.1.call-start = ((), (), s32[]{:S(2)}) async-start(), calls=%async_computation.3 | async-start | bytes 5242880 | tf_op jit(solution)/shard_map/reduce_scatter | solution.py:63
  312.9 7.8 %copy-start.1 = (s32[1024]{0:T(1024)S(1)}, s32[1024]{0:T(1024)}, u32[]{:S(2)}) copy-start(s32[1024]{0:T(1024)} %param.7) | copy-start | bytes 12292
Sparse Core Ops, SparseCore 0:
  73.9 158.5 all-reduce.2
  237.1 23.8 reduce-scatter.4
  263.5 44.5 reduce-scatter.2
where the time goes:
time: 330 us; the launch traced here: 327 us
  waiting for transfers between devices  192 us (58%)
  local copies, waits for them, and re-layouts  62.6 us (19%)
  other arithmetic  20.2 us (6%)
  matrix products  19.6 us (6%)
  blocking collectives  18.6 us (6%)
  between operations  14 us (4%)
    psum x1, waiting for transfers between devices, shards(): col_embed = lax.psum(partial_value, 'tp').astype(jnp.float32)  156 us
    gather x1, local copies, waits for them, and re-layouts, shards(): picked = jnp.take(table, jnp.clip(local_ids, 0, vocab_here - 1), axis=0)  51.9 us
    reduce_scatter x1, waiting for transfers between devices, shards(): lax.psum_scatter(query_term, 'ctx', scatter_dimension=0, tiled=True)  32.9 us
    dot_general x1, matrix products, shards(): jnp.dot(col_scaled, w_query, preferred_element_type=jnp.float32)  9.92 us
  transfers between devices with their start and end apart: 3, of which 3 were waited for; matrix products, arithmetic and copies ran while one was open for 6% of the time, Pallas kernels for 0%

commit v1 on v0

v1 whole, which is shorter than its diff:
```python
import functools

import jax
import jax.numpy as jnp
from jax import lax
from jax.experimental import pallas as pl
from jax.experimental.pallas import tpu as pltpu
from jax.sharding import PartitionSpec as P

HEADS = 64
KV_HEADS = 8
HD = 128
BLOCK = 128
GROUP_ROWS = 8
MESH = pl.DeviceIdType.MESH
VMEM_SPEC = pl.BlockSpec(memory_space=pltpu.VMEM)
VMEM_LIMIT = 60 * 1024 * 1024


rotary_base = 500000.0


def greet(axis, others):
    barrier = pltpu.get_barrier_semaphore()
    for other in others:
        pl.semaphore_signal(barrier, inc=1, device_id={axis: other}, device_id_type=MESH)
    pl.semaphore_wait(barrier, len(others))


def pick_kernel(group_ref, table_ref, lane_ref, out_ref, held, sem):
    count = out_ref.shape[0]

    @pl.loop(0, count, unroll=8)
    def _(k):
        source = pl.multiple_of(group_ref[k] * GROUP_ROWS, GROUP_ROWS)
        target = pl.multiple_of(k * GROUP_ROWS, GROUP_ROWS)
        pltpu.make_async_copy(
            table_ref.at[pl.ds(source, GROUP_ROWS)], held.at[pl.ds(target, GROUP_ROWS)], sem
        ).start()

    pltpu.make_async_copy(table_ref.at[pl.ds(0, count * GROUP_ROWS)], held, sem).wait()
    tile = min(count, 128)
    for at in range(0, count, tile):
        row = lax.broadcasted_iota(jnp.int32, (tile, tile * GROUP_ROWS), 0) * GROUP_ROWS
        column = lax.broadcasted_iota(jnp.int32, (tile, tile * GROUP_ROWS), 1)
        choose = (column == row + lane_ref[at : at + tile, :1]).astype(jnp.float32).astype(jnp.bfloat16)
        out_ref[at : at + tile] = jnp.dot(
            choose,
            held[at * GROUP_ROWS : (at + tile) * GROUP_ROWS],
            preferred_element_type=jnp.float32,
        ).astype(out_ref.dtype)


def pick_rows(table, local_ids):
    count = local_ids.shape[0]
    columns = table.shape[1]
    lane = jnp.broadcast_to((local_ids % GROUP_ROWS)[:, None], (count, 128))
    return pl.pallas_call(
        pick_kernel,
        out_shape=jax.ShapeDtypeStruct((count, columns), table.dtype),
        grid_spec=pltpu.PrefetchScalarGridSpec(
            num_scalar_prefetch=1,
            grid=(),
            in_specs=[pl.BlockSpec(memory_space=pl.ANY), VMEM_SPEC],
            out_specs=VMEM_SPEC,
            scratch_shapes=[
                pltpu.VMEM((count * GROUP_ROWS, columns), table.dtype),
                pltpu.SemaphoreType.DMA,
            ],
        ),
    )(local_ids // GROUP_ROWS, table, lane)


def spread_kernel(ring, x_ref, out_ref, own_sem, send_sem, recv_sem):
    me = lax.axis_index("tp")
    at, side = me // 2, lax.rem(me, 2)
    up = lax.rem(at + 1, ring) * 2 + side
    down = lax.rem(at + ring - 1, ring) * 2 + side
    across = at * 2 + 1 - side
    greet("tp", (up, down, across))
    part = x_ref.shape[0] // 4
    last = ring - 1
    own = pltpu.make_async_copy(x_ref, out_ref.at[me], own_sem)
    own.start()
    sends = []

    def slot(back, other, q):
        origin = lax.rem(at + ring - back, ring) * 2 + (1 - side if other else side)
        return out_ref.at[origin, pl.ds(q * part, part)]

    def copy(back, other, q, way):
        here = slot(back, other, q)
        source = x_ref.at[pl.ds(q * part, part)] if (back, other) == (0, 0) else here
        target = {"up": up, "down": down, "across": across}[way]
        lands = {
            "up": ((back + 1) % ring, other),
            "down": ((back + last) % ring, other),
            "across": (back, 1 - other),
        }[way]
        number = len(sends)
        sent = pltpu.make_async_remote_copy(
            src_ref=source,
            dst_ref=here,
            send_sem=send_sem.at[number],
            recv_sem=recv_sem.at[lands[0] * 2 + lands[1], q],
            device_id={"tp": target},
            device_id_type=MESH,
        )
        sent.start()
        sends.append(sent)

    seen = set()

    def arrive(back, other, q):
        seen.add((back, other, q))
        here = slot(back, other, q)
        pltpu.make_async_copy(here, here, recv_sem.at[back * 2 + other, q]).wait()

    for q in (0, 1):
        copy(0, 0, q, "across")
    for q in (2, 3):
        copy(0, 0, q, "up")
        copy(0, 0, 5 - q, "down")
    for q in (0, 1):
        copy(0, 0, q, "up")
        copy(0, 0, 1 - q, "down")
    for q in (2, 3):
        copy(0, 0, q, "across")
    arrive(0, 1, 0)
    copy(0, 1, 0, "up")
    copy(0, 1, 0, "down")
    arrive(1, 0, 2)
    copy(1, 0, 2, "up")
    copy(1, 0, 2, "across")
    arrive(last, 0, 3)
    copy(last, 0, 3, "down")
    copy(last, 0, 3, "across")
    arrive(0, 1, 1)
    copy(0, 1, 1, "up")
    copy(0, 1, 1, "down")
    arrive(1, 0, 3)
    copy(1, 0, 3, "across")
    arrive(last, 0, 2)
    copy(last, 0, 2, "across")
    arrive(1, 0, 0)
    copy(1, 0, 0, "up")
    arrive(last, 0, 1)
    copy(last, 0, 1, "down")
    for q in (2, 3):
        arrive(2, 0, q)
        copy(2, 0, q, "across")
    arrive(1, 1, 0)
    copy(1, 1, 0, "up")
    arrive(last, 1, 1)
    copy(last, 1, 1, "down")
    for back in range(ring):
        for other in (0, 1):
            for q in range(4):
                if (back, other) != (0, 0) and (back, other, q) not in seen:
                    arrive(back, other, q)
    own.wait()
    for sent in sends:
        sent.wait_send()


def spread(rows, collective_id):
    tp_count = lax.axis_size("tp")
    count, columns = rows.shape
    ring = tp_count // 2
    if ring != 4 or count % 64:
        return lax.all_gather(rows, "tp", axis=0, tiled=True)
    out = pl.pallas_call(
        functools.partial(spread_kernel, ring),
        out_shape=jax.ShapeDtypeStruct((tp_count, count, columns), rows.dtype),
        in_specs=[VMEM_SPEC],
        out_specs=VMEM_SPEC,
        scratch_shapes=[
            pltpu.SemaphoreType.DMA,
            pltpu.SemaphoreType.DMA((28,)),
            pltpu.SemaphoreType.DMA((tp_count, 4)),
        ],
        compiler_params=pltpu.CompilerParams(
            collective_id=collective_id, has_side_effects=True, vmem_limit_bytes=VMEM_LIMIT
        ),
    )(rows)
    return out.reshape(tp_count * count, columns)


def fold_kernel(n, pieces, arrays, *refs):
    parts, outs = refs[:arrays], refs[arrays : 2 * arrays]
    near, far = refs[2 * arrays : 3 * arrays], refs[3 * arrays : 4 * arrays]
    near_send, near_recv, far_send, far_recv = refs[4 * arrays :]
    chips = n // 2
    me = lax.axis_index("ctx")
    chip, core = me // 2, lax.rem(me, 2)
    mate = chip * 2 + 1 - core
    remote = [lax.rem(chip + step, chips) * 2 + core for step in range(1, chips)]
    greet("ctx", [mate] + remote)
    sends = []

    def give(index, step):
        which, low, size = pieces[index]
        target = lax.rem(chip + step, chips) * 2 + 1 - core
        sent = pltpu.make_async_remote_copy(
            src_ref=parts[which].at[target, pl.ds(low, size)],
            dst_ref=near[which].at[step, pl.ds(low, size)],
            send_sem=near_send.at[index, step],
            recv_sem=near_recv.at[index, step],
            device_id={"ctx": mate},
            device_id_type=MESH,
        )
        sent.start()
        sends.append(sent)
        return sent

    handed = {}
    for step in list(range(1, chips)) + [0]:
        for index in range(len(pieces)):
            handed[index, step] = give(index, step)
    crossed = {}
    for index, (which, low, size) in enumerate(pieces):
        rows = pl.ds(low, size)
        for step in range(1, chips):
            target = remote[step - 1]
            handed[index, step].wait_recv()
            near[which][step, rows] = near[which][step, rows] + parts[which][target, rows]
            sent = pltpu.make_async_remote_copy(
                src_ref=near[which].at[step, rows],
                dst_ref=far[which].at[step, rows],
                send_sem=far_send.at[index, step],
                recv_sem=far_recv.at[index, step],
                device_id={"ctx": target},
                device_id_type=MESH,
            )
            sent.start()
            sends.append(sent)
            crossed[index, step] = sent
    for index, (which, low, size) in enumerate(pieces):
        rows = pl.ds(low, size)
        handed[index, 0].wait_recv()
        total = parts[which][me, rows] + near[which][0, rows]
        for step in range(1, chips):
            crossed[index, step].wait_recv()
            total = total + far[which][step, rows]
        outs[which][rows] = total
    for sent in sends:
        sent.wait_send()


def fold(*arrays):
    n = arrays[0].shape[0]
    chips = n // 2
    pieces = []
    for which, array in enumerate(arrays):
        size = array.shape[1]
        cut = size // 4 if size * array.shape[2] > 131072 else size
        pieces += [(which, low, cut) for low in range(0, size, cut)]
    sems = pltpu.SemaphoreType.DMA((len(pieces), chips))
    slots = [pltpu.VMEM((chips,) + a.shape[1:], a.dtype) for a in arrays]
    return pl.pallas_call(
        functools.partial(fold_kernel, n, tuple(pieces), len(arrays)),
        out_shape=[jax.ShapeDtypeStruct(a.shape[1:], a.dtype) for a in arrays],
        in_specs=[VMEM_SPEC] * len(arrays),
        out_specs=[VMEM_SPEC] * len(arrays),
        scratch_shapes=slots + slots + [sems] * 4,
        compiler_params=pltpu.CompilerParams(
            collective_id=2, has_side_effects=True, vmem_limit_bytes=VMEM_LIMIT
        ),
    )(*arrays)


def share_kernel(n, x_ref, out_ref, own_sem, send_sem, recv_sem):
    me = lax.axis_index("ctx")
    greet("ctx", [lax.rem(me + step, n) for step in range(1, n)])
    own = pltpu.make_async_copy(x_ref, out_ref.at[me], own_sem)
    own.start()
    copies = []
    for step in range(1, n):
        copy = pltpu.make_async_remote_copy(
            src_ref=x_ref,
            dst_ref=out_ref.at[me],
            send_sem=send_sem.at[step],
            recv_sem=recv_sem.at[step],
            device_id={"ctx": lax.rem(me + step, n)},
            device_id_type=MESH,
        )
        copy.start()
        copies.append(copy)
    for step in range(1, n):
        lands = out_ref.at[lax.rem(me + n - step, n)]
        pltpu.make_async_copy(lands, lands, recv_sem.at[step]).wait()
    own.wait()
    for copy in copies:
        copy.wait_send()


def share(rows):
    n = lax.axis_size("ctx")
    out = pl.pallas_call(
        functools.partial(share_kernel, n),
        out_shape=jax.ShapeDtypeStruct((n,) + rows.shape, rows.dtype),
        in_specs=[VMEM_SPEC],
        out_specs=VMEM_SPEC,
        scratch_shapes=[
            pltpu.SemaphoreType.DMA,
            pltpu.SemaphoreType.DMA((n,)),
            pltpu.SemaphoreType.DMA((n,)),
        ],
        compiler_params=pltpu.CompilerParams(collective_id=3, has_side_effects=True),
    )(rows)
    return out.reshape(n * rows.shape[0], rows.shape[1])


def rotary(values_in, pos_rows):
    half_dim = values_in.shape[-1] // 2
    steps_up = jnp.arange(half_dim, dtype=jnp.float32)
    freqs = jnp.power(rotary_base, -2.0 * steps_up / values_in.shape[-1])
    angle = pos_rows.astype(jnp.float32)[:, None] * freqs[None, :]
    angle = angle.reshape((angle.shape[0],) + (1,) * (values_in.ndim - 2) + (half_dim,))
    cosine = jnp.cos(angle)
    sine = jnp.sin(angle)
    first = values_in[..., :half_dim]
    second = values_in[..., half_dim:]
    return jnp.concatenate(
        [first * cosine - second * sine, second * cosine + first * sine], axis=-1
    )


def document_of(pos_rows, doc_lengths):
    ends = jnp.cumsum(doc_lengths)
    return jnp.sum((ends[None, :] <= pos_rows[:, None]).astype(jnp.int32), axis=1)


def plan(token_ids, vocab_here, capacity):
    tokens_all = token_ids.shape[0]
    order = jnp.arange(tokens_all, dtype=jnp.int32)
    same = token_ids[:, None] == token_ids[None, :]
    first = jnp.min(jnp.where(same, order[None, :], tokens_all), axis=1)
    shard = token_ids // vocab_here
    leads = first == order
    before = (order[None, :] < first[:, None]) & leads[None, :] & (shard[None, :] == shard[:, None])
    rank = jnp.sum(before.astype(jnp.int32), axis=1)
    most = jnp.max(rank) + 1
    return shard, rank, leads, (most + capacity - 1) // capacity


def shards(token_ids, doc_lengths, block_order, table, gain, w_query, w_keyval):
    ctx_count = lax.axis_size("ctx")
    ctx_at = lax.axis_index("ctx")
    tp_count = lax.axis_size("tp")
    tp_at = lax.axis_index("tp")
    tokens_all = token_ids.shape[0]
    tok_here = tokens_all // ctx_count
    vocab_here = table.shape[0]
    columns = table.shape[1]
    width = gain.shape[0]
    heads_here = HEADS // tp_count
    blocks = tokens_all // BLOCK
    capacity = tokens_all // tp_count
    positions = (
        block_order[:, None] * BLOCK + jnp.arange(BLOCK, dtype=jnp.int32)[None, :]
    ).reshape(tokens_all)

    def redeal(values):
        pick = block_order[:, None] == jnp.arange(blocks, dtype=jnp.int32)[None, :]
        spread_out = jnp.where(pick[:, :, None], values.reshape(1, blocks, BLOCK), 0)
        return jnp.sum(spread_out, axis=1).reshape(tokens_all)

    shard, rank, leads, rounds = plan(token_ids, vocab_here, capacity)
    local_ids = token_ids - tp_at * vocab_here
    mine = leads & (shard == tp_at)
    row_shard, row_rank = redeal(shard), redeal(rank)

    def one_round(number, collective_id):
        wanted = number * capacity + jnp.arange(capacity, dtype=jnp.int32)
        hit = mine[None, :] & (rank[None, :] == wanted[:, None])
        asked = jnp.sum(jnp.where(hit, local_ids[None, :], 0), axis=1)
        gathered = spread(pick_rows(table, asked), collective_id)
        in_round = (row_rank >= number * capacity) & (row_rank < (number + 1) * capacity)
        slot = jnp.where(in_round, row_shard * capacity + row_rank - number * capacity, -1)
        choose = slot[:, None] == jnp.arange(tp_count * capacity, dtype=jnp.int32)[None, :]
        return jnp.dot(
            choose.astype(table.dtype), gathered, preferred_element_type=jnp.float32
        ).astype(table.dtype)

    embed = one_round(0, 0)
    embed = lax.fori_loop(1, rounds, lambda i, held: held + one_round(i, 1), embed)
    col_embed = embed.astype(jnp.float32)
    kv_head = tp_at * heads_here // (HEADS // KV_HEADS)
    w_pair = lax.dynamic_slice_in_dim(w_keyval, kv_head * HD, HD, 2).reshape(
        w_keyval.shape[0], 2 * HD
    )
    gain_here = lax.dynamic_slice_in_dim(gain, ctx_at * columns, columns)
    col_scaled = (col_embed * gain_here).astype(jnp.bfloat16)
    query_term = jnp.dot(col_scaled, w_query, preferred_element_type=jnp.float32)
    pair_term = jnp.dot(col_scaled, w_pair, preferred_element_type=jnp.float32)
    square_term = jnp.sum(col_embed * col_embed, axis=1)
    pair_raw, query_raw, sumsq = fold(
        pair_term.reshape(ctx_count, tok_here, 2 * HD),
        query_term.reshape(ctx_count, tok_here, heads_here * HD),
        jnp.broadcast_to(square_term.reshape(ctx_count, 1, tok_here), (ctx_count, 8, tok_here)),
    )
    inverse = lax.rsqrt(sumsq[0] / width + 1e-05)
    my_pos = lax.dynamic_slice_in_dim(positions, ctx_at * tok_here, tok_here)
    query_rows = rotary(
        (query_raw * inverse[:, None]).reshape(tok_here, heads_here, HD), my_pos
    ).astype(jnp.bfloat16)
    key_rows = rotary(pair_raw[:, :HD] * inverse[:, None], my_pos).astype(jnp.bfloat16)
    value_rows = (pair_raw[:, HD:] * inverse[:, None]).astype(jnp.bfloat16)
    my_doc = document_of(my_pos, doc_lengths)
    stacked = jnp.transpose(query_rows, (1, 0, 2)).reshape(heads_here * tok_here, HD)
    query_pos = jnp.tile(my_pos, heads_here)
    query_doc = jnp.tile(my_doc, heads_here)
    inv_root = 1.0 / jnp.sqrt(jnp.float32(HD))
    shared = share(jnp.concatenate([key_rows, value_rows], axis=1))
    key_piece, value_piece = shared[:, :HD], shared[:, HD:]
    key_doc = document_of(positions, doc_lengths)
    allowed = (key_doc[None, :] == query_doc[:, None]) & (positions[None, :] <= query_pos[:, None])
    scores = (
        lax.dot_general(
            stacked, key_piece, (((1,), (1,)), ((), ())), preferred_element_type=jnp.float32
        )
        * inv_root
    )
    masked = jnp.where(allowed, scores, jnp.float32(-1e30))
    largest = jnp.max(masked, axis=1)
    weights = jnp.where(allowed, jnp.exp(masked - largest[:, None]), jnp.float32(0.0))
    totals = jnp.sum(weights, axis=1)
    accum = jnp.dot(weights.astype(jnp.bfloat16), value_piece, preferred_element_type=jnp.float32)
    mixed = (accum / totals[:, None]).reshape(heads_here, tok_here, HD)
    return jnp.transpose(mixed, (1, 0, 2)).reshape(tok_here, heads_here * HD).astype(jnp.bfloat16)


def solution(mesh):
    in_specs = (P(), P(), P(), P("tp", "ctx"), P(), P("ctx", "tp"), P("ctx", None, None))
    out_specs = P("ctx", "tp")
    return jax.shard_map(shards, mesh=mesh, in_specs=in_specs, out_specs=out_specs, check_vma=False)
```

time: 330 us -> 163 us (0.49)
  waiting for transfers between devices: 192 us -> 0 us
  Pallas kernels: 0 us -> 113 us
  local copies, waits for them, and re-layouts: 62.6 us -> 6.06 us
  blocking collectives: 18.6 us -> 0 us
  between operations: 14 us -> 0.92 us
  matrix products: 19.6 us -> 24 us
    psum x1 -> x0, waiting for transfers between devices: 156 us -> none  [shards(): col_embed = lax.psum(partial_value, 'tp').astype(jnp.float32)]
    pallas_call x0 -> x4, Pallas kernels: none -> 113 us  [the longest x1 57 us: spread(): pl.pallas_call(functools.partial(spread_kernel, ring), out_shape=jax.Shap...]
    gather x3 -> x0, local copies, waits for them, and re-layouts: 58 us -> none  [the longest x1 51.9 us: shards(): picked = jnp.take(table, jnp.clip(local_ids, 0, vocab_here - 1), axis=0)]
    reduce_scatter x2 -> x0, waiting for transfers between devices: 35.9 us -> none  [the longest x1 32.9 us: shards(): lax.psum_scatter(query_term, 'ctx', scatter_dimension=0, tiled=True)]
    all_gather x2 -> x0, blocking collectives: 12.5 us -> none  [the longest x1 6.45 us: shards(): key_piece = lax.all_gather(key_rows, 'ctx', axis=0, tiled=True)]
    dot_general x0 -> x1, matrix products: none -> 8.42 us  [one_round(): jnp.dot(choose.astype(table.dtype), gathered, preferred_element_type=jnp....]
    unnamed x1 -> x0, blocking collectives: 6.12 us -> none
    gather x4 -> x0, other arithmetic: 4.33 us -> none  [the longest x2 4.32 us: shards(): positions = block_order[row_index // BLOCK] * BLOCK + row_index % BLOCK]
  transfers between devices with their start and end apart: 3 -> 0, of which waited for: 3 -> 0; matrix products, arithmetic and copies ran while one was open for 6% -> 0% of each run, Pallas kernels for 0% -> 0%
where the time goes in v1:
time: 163 us
  Pallas kernels  113 us (69%)
  matrix products  24 us (15%)
  other arithmetic  19.1 us (12%)
  local copies, waits for them, and re-layouts  6.06 us (4%)
    pallas_call x1, Pallas kernels, spread(): pl.pallas_call(functools.partial(spread_kernel, ring), out_shape=jax.Shap...  57 us
    pallas_call x1, Pallas kernels, fold(): pl.pallas_call(functools.partial(fold_kernel, n, tuple(pieces), len(array...  38.7 us
    pallas_call x1, Pallas kernels, share(): pl.pallas_call(functools.partial(share_kernel, n), out_shape=jax.ShapeDty...  10.4 us
    dot_general x1, matrix products, one_round(): jnp.dot(choose.astype(table.dtype), gathered, preferred_element_type=jnp....  8.42 us
    pallas_call x1, Pallas kernels, pick_rows(): pl.pallas_call(pick_kernel, out_shape=jax.ShapeDtypeStruct((count, column...  6.35 us
    dot_general x1, matrix products, shards(): jnp.dot(col_scaled, w_query, preferred_element_type=jnp.float32)  6.05 us
    dot_general x1, matrix products, shards(): pair_term = jnp.dot(col_scaled, w_pair, preferred_element_type=jnp.float32)  4.51 us
    reduce_sum x1, other arithmetic, shards(): totals = jnp.sum(weights, axis=1)  3.82 us

profile of v1, /device:TPU:1, one launch (start us, length us, event | category | flops | bytes accessed | tf_op | source)
XLA Modules:
  0.0 162.6 jit_solution(9409065117030939755)
XLA Ops:
  0.0 1.5 select_reduce_fusion.1
  1.5 0.7 compare_and_fusion.1
  2.3 1.5 convert_reduce_fusion
  3.7 0.6 reduce_max.18
  5.0 0.7 broadcast_subtract_fusion
  5.7 0.2 select_reduce_fusion.2
  5.9 0.6 and_select_fusion.2
  6.5 0.7 broadcast_in_dim.157.lane_ref
  7.2 6.3 %shard_map.73.x_ref = bf16[128,2048]{1,0:T(8,128)(2,1)} custom-call(s32[128]{0:T(128)} %get-tuple-element.170.group_ref, bf16[16032,2048]{1,0:T(8,128)(2,1)} %table_ref.1, s32[128,128]{1,0:T(8,128)} %broadcast_in_dim.157.lane_ref), custom_call_target="tpu_custom_call" | custom-call | tf_op jit(solution)/shard_map/pallas_call | solution.py:58
  13.5 0.0 copy-start.3
  13.6 57.0 %shard_map.74 = bf16[8,128,2048]{2,1,0:T(8,128)(2,1)} custom-call(bf16[128,2048]{1,0:T(8,128)(2,1)} %shard_map.73.x_ref), custom_call_target="tpu_custom_call" | custom-call | tf_op jit(solution)/shard_map/pallas_call | solution.py:172
  70.6 0.0 copy-done.3
  70.6 0.1 iota_compare_fusion.11
  70.7 0.1 select_reduce_fusion.4
  70.8 8.4 %fusion.12 = bf16[1024,2048]{1,0:T(8,128)(2,1)} fusion(bf16[1024,2048]{1,0:T(8,128)(2,1)} %bitcast.49, s32[1024]{0:T(1024)S(1)} %add_select_fusion.1), kind=kOutput, calls=%fused_computation.30 | convolution fusion | flops 4298113024 | bytes 8392704 | tf_op jit(solution)/shard_map/dot_general | solution.py:382
  79.2 0.7 dynamic_slice.10
  79.9 0.0 copy-start.2
  79.9 3.6 %fusion.3 = (f32[1024]{0:T(1024)S(1)}, bf16[1024,2048]{1,0:T(8,128)(2,1)S(1)}) fusion(bf16[1024,2048]{1,0:T(8,128)(2,1)} %get-tuple-element.126, f32[2048]{0:T(1024)S(1)} %dynamic_slice.10), kind=kLoop, calls=%fused_computation.15 | loop fusion | flops 10484736 | bytes 8400896 | tf_op jit(solution)/shard_map/reduce_sum | solution.py:397
  83.6 0.0 copy-start
  83.6 0.0 copy-done.2
  83.6 6.0 %fusion.31 = f32[1024,1024]{1,0:T(8,128)} fusion(bf16[1024,2048]{1,0:T(8,128)(2,1)S(1)} %get-tuple-element.158, bf16[2048,1024]{1,0:T(8,128)(2,1)S(1)} %copy-done.2), kind=kOutput, calls=%fused_computation.83 | convolution fusion | flops 4294967296 | bytes 12582912 | tf_op jit(solution)/shard_map/dot_general | solution.py:395
  89.6 0.0 copy-done
  89.6 1.8 %constant_dynamic-slice_fusion = bf16[2048,2,128]{2,1,0:T(2,128)(2,1)S(1)} fusion(bf16[2048,2,1024]{2,1,0:T(2,128)(2,1)} %param.15, s32[]{:T(128)S(6)} %select_n.118), kind=kLoop, calls=%fused_computation.76 | loop fusion | bytes 2097156 | tf_op jit(solution)/shard_map/dynamic_slice | solution.py:390
  91.5 0.7 reshape.279
  92.2 4.5 %fusion.30.refs_0_ = f32[4,256,256]{2,1,0:T(8,128)} fusion(bf16[4,256,2048]{2,1,0:T(8,128)(2,1)} %bitcast.50, bf16[2048,256,1]{1,0,2:T(8,128)(2,1)S(1)} %reshape.279), kind=kOutput, calls=%fused_computation.82 | convolution fusion | flops 1073741824 | bytes 6291456 | tf_op jit(solution)/shard_map/dot_general | solution.py:396
  96.7 0.0 copy-start.4
  96.7 0.6 broadcast_in_dim.159.refs_2_
  97.3 38.7 %shard_map.75 = (f32[256,256]{1,0:T(8,128)}, f32[256,1024]{1,0:T(8,128)}, f32[8,256]{1,0:T(8,128)}) custom-call(f32[4,256,256]{2,1,0:T(8,128)} %fusion.30.refs_0_, f32[4,256,1024]{2,1,0:T(8,128)} %bitcast.48, f32[4,8,256]{2,1,0:T(8,128)} %broadcast_in_dim.159.refs_2_), custom_call_target="tpu_custom_call" | custom-call | tf_op jit(solution)/shard_map/pallas_call | solution.py:260
  136.1 0.7 add_rsqrt_fusion
  136.8 1.1 slice_multiply_fusion
  137.8 0.0 copy-done.4
  137.9 0.1 add_bitcast_fusion
  137.9 0.1 fusion.28
  138.0 0.6 subtract_convert_fusion.1
  138.6 0.8 pad_maximum_fusion.1.x_ref
  139.4 10.4 %shard_map.76 = bf16[4,256,256]{2,1,0:T(8,128)(2,1)} custom-call(bf16[256,256]{1,0:T(8,128)(2,1)} %pad_maximum_fusion.1.x_ref), custom_call_target="tpu_custom_call" | custom-call | tf_op jit(solution)/shard_map/pallas_call | solution.py:299
  149.8 1.4 multiply_bitcast_fusion
  151.1 0.2 copy.20
  151.3 0.0 copy-start.5
  151.3 0.0 copy-start.1
  151.3 0.3 fusion.29
  151.7 0.4 subtract_convert_fusion
  152.1 0.3 pad_maximum_fusion
  152.4 0.0 copy-done.5
  152.4 0.2 reduce-window.8
  152.6 0.1 convert_reduce_fusion.2
  152.7 0.1 convert_reduce_fusion.1
  152.8 0.0 copy-done.1
  152.8 2.1 %fusion.4 = (f32[2048]{0:T(1024)S(1)}, f32[2048,1024]{0,1:T(8,128)S(1)}) fusion(s32[2048]{0:T(1024)S(1)} %bitcast.61, s32[2048]{0:T(1024)S(1)} %bitcast.58, s32[1024]{0:T(1024)S(1)} %add_bitcast_fusion, s32[1024]{0:T(1024)S(1)} %convert_reduce_fusion.1, bf16[2048,128]{1,0:T(8,128)(2,1)S(1)} %bitcast.51, bf16[1024,256]{1,0:T(8,128)(2,1)S(1)} %bitcast.52), kind=kOutput, calls=%fused_computation.19 | convolution fusion | flops 549451776 | bytes 9207808 | tf_op jit(solution)/shard_map/dot_general | solution.py:420
  154.9 3.8 %fusion.5 = f32[2048]{0:T(1024)S(1)} fusion(f32[2048,1024]{0,1:T(8,128)S(1)} %get-tuple-element.172, f32[2048]{0:T(1024)S(1)} %get-tuple-element.171, s32[2048]{0:T(1024)S(1)} %bitcast.62, s32[2048]{0:T(1024)S(1)} %bitcast.59, s32[1024]{0:T(1024)S(1)} %add_bitcast_fusion, s32[1024]{0:T(1024)S(1)} %convert_reduce_fusion.1), kind=kLoop, calls=%fused_computation.20 | loop fusion | flops 16775168 | bytes 8429568 | tf_op jit(solution)/shard_map/reduce_sum | solution.py:428
  158.7 2.9 %fusion.17 = bf16[2048,128]{1,0:T(8,128)(2,1)S(1)} fusion(f32[2048,1024]{0,1:T(8,128)S(1)} %get-tuple-element.172, f32[2048]{0:T(1024)S(1)} %get-tuple-element.171, s32[2048]{0:T(1024)S(1)} %bitcast.63, s32[2048]{0:T(1024)S(1)} %bitcast.60, s32[1024]{0:T(1024)S(1)} %add_bitcast_fusion, s32[1024]{0:T(1024)S(1)} %convert_reduce_fusion.1, ...), kind=kOutput, calls=%fused_computation.33 | convolution fusion | flops 554172416 | bytes 9216000 | tf_op jit(solution)/shard_map/dot_general | solution.py:429
  161.6 0.9 copy.26
  (9 shorter events, 0.1 us)
Async XLA Ops:
  13.5 57.1 %copy-start.3 = (s32[8]{0:T(128)S(1)}, s32[8]{0:T(128)}, u32[]{:S(2)}) copy-start(s32[8]{0:T(128)} %param.11) | copy-start | bytes 100
  79.9 3.7 %copy-start.2 = (bf16[2048,1024]{1,0:T(8,128)(2,1)S(1)}, bf16[2048,1024]{1,0:T(8,128)(2,1)}, u32[]{:S(2)}) copy-start(bf16[2048,1024]{1,0:T(8,128)(2,1)} %param.14) | copy-start | bytes 12582916
  83.6 6.1 %copy-start = (bf16[1024,2048]{1,0:T(8,128)(2,1)}, bf16[1024,2048]{1,0:T(8,128)(2,1)S(1)}, u32[]{:S(2)}) copy-start(bf16[1024,2048]{1,0:T(8,128)(2,1)S(1)} %get-tuple-element.158) | copy-start | bytes 12582916
  96.7 41.2 %copy-start.4 = (s32[8]{0:T(128)S(1)}, s32[8]{0:T(128)}, u32[]{:S(2)}) copy-start(s32[8]{0:T(128)} %param.11) | copy-start | bytes 100
  151.3 1.1 copy-start.5
  151.3 1.5 copy-start.1

commit v2 on v1

--- a/solution.py
+++ b/solution.py
@@ -71,119 +71,209 @@
     )(local_ids // GROUP_ROWS, table, lane)
 
 
-def spread_kernel(ring, x_ref, out_ref, own_sem, send_sem, recv_sem):
+def spread_kernel(line, x_ref, out_ref, own_sem, send_sem, recv_sem):
     me = lax.axis_index("tp")
     at, side = me // 2, lax.rem(me, 2)
-    up = lax.rem(at + 1, ring) * 2 + side
-    down = lax.rem(at + ring - 1, ring) * 2 + side
+    last = line - 1
+    up = jnp.minimum(at + 1, last) * 2 + side
+    down = jnp.maximum(at - 1, 0) * 2 + side
     across = at * 2 + 1 - side
-    greet("tp", (up, down, across))
-    part = x_ref.shape[0] // 4
-    last = ring - 1
+    barrier = pltpu.get_barrier_semaphore()
+
+    def hail(other):
+        pl.semaphore_signal(barrier, inc=1, device_id={"tp": other}, device_id_type=MESH)
+
+    hail(across)
+    pl.when(at < last)(lambda: hail(up))
+    pl.when(at > 0)(lambda: hail(down))
+    inner = (at > 0) & (at < last)
+    pl.when(inner)(lambda: pl.semaphore_wait(barrier, 3))
+    pl.when(jnp.logical_not(inner))(lambda: pl.semaphore_wait(barrier, 2))
+
+    unit = x_ref.shape[0] // 8
+    pieces = [(0, 1), (1, 2), (3, 2), (5, 2), (7, 1)]
+    pair_first, line_first = (0, 1), (2, 3, 4)
     own = pltpu.make_async_copy(x_ref, out_ref.at[me], own_sem)
     own.start()
     sends = []
 
-    def slot(back, other, q):
-        origin = lax.rem(at + ring - back, ring) * 2 + (1 - side if other else side)
-        return out_ref.at[origin, pl.ds(q * part, part)]
-
-    def copy(back, other, q, way):
-        here = slot(back, other, q)
-        source = x_ref.at[pl.ds(q * part, part)] if (back, other) == (0, 0) else here
+    def view(ref, q):
+        low, size = pieces[q]
+        return ref.at[pl.ds(low * unit, size * unit)]
+
+    def start(origin, q, way, condition, mine=False):
         target = {"up": up, "down": down, "across": across}[way]
-        lands = {
-            "up": ((back + 1) % ring, other),
-            "down": ((back + last) % ring, other),
-            "across": (back, 1 - other),
-        }[way]
-        number = len(sends)
-        sent = pltpu.make_async_remote_copy(
-            src_ref=source,
-            dst_ref=here,
-            send_sem=send_sem.at[number],
-            recv_sem=recv_sem.at[lands[0] * 2 + lands[1], q],
+        copy = pltpu.make_async_remote_copy(
+            src_ref=view(x_ref if mine else out_ref.at[origin], q),
+            dst_ref=view(out_ref.at[origin], q),
+            send_sem=send_sem.at[len(sends)],
+            recv_sem=recv_sem.at[origin, q],
             device_id={"tp": target},
             device_id_type=MESH,
         )
-        sent.start()
-        sends.append(sent)
-
-    seen = set()
-
-    def arrive(back, other, q):
-        seen.add((back, other, q))
-        here = slot(back, other, q)
-        pltpu.make_async_copy(here, here, recv_sem.at[back * 2 + other, q]).wait()
-
-    for q in (0, 1):
-        copy(0, 0, q, "across")
-    for q in (2, 3):
-        copy(0, 0, q, "up")
-        copy(0, 0, 5 - q, "down")
-    for q in (0, 1):
-        copy(0, 0, q, "up")
-        copy(0, 0, 1 - q, "down")
-    for q in (2, 3):
-        copy(0, 0, q, "across")
-    arrive(0, 1, 0)
-    copy(0, 1, 0, "up")
-    copy(0, 1, 0, "down")
-    arrive(1, 0, 2)
-    copy(1, 0, 2, "up")
-    copy(1, 0, 2, "across")
-    arrive(last, 0, 3)
-    copy(last, 0, 3, "down")
-    copy(last, 0, 3, "across")
-    arrive(0, 1, 1)
-    copy(0, 1, 1, "up")
-    copy(0, 1, 1, "down")
-    arrive(1, 0, 3)
-    copy(1, 0, 3, "across")
-    arrive(last, 0, 2)
-    copy(last, 0, 2, "across")
-    arrive(1, 0, 0)
-    copy(1, 0, 0, "up")
-    arrive(last, 0, 1)
-    copy(last, 0, 1, "down")
-    for q in (2, 3):
-        arrive(2, 0, q)
-        copy(2, 0, q, "across")
-    arrive(1, 1, 0)
-    copy(1, 1, 0, "up")
-    arrive(last, 1, 1)
-    copy(last, 1, 1, "down")
-    for back in range(ring):
-        for other in (0, 1):
-            for q in range(4):
-                if (back, other) != (0, 0) and (back, other, q) not in seen:
-                    arrive(back, other, q)
+        sends.append((condition, copy))
+        if condition is None:
+            copy.start()
+        else:
+            pl.when(condition)(copy.start)
+
+    def arrive(origin, q, condition):
+        here = view(out_ref.at[origin], q)
+        wait = pltpu.make_async_copy(here, here, recv_sem.at[origin, q]).wait
+        if condition is None:
+            wait()
+        else:
+            pl.when(condition)(wait)
+
+    for q in pair_first:
+        start(me, q, "across", None, True)
+    for q in line_first + pair_first:
+        start(me, q, "up", at < last, True)
+        start(me, q, "down", at > 0, True)
+    for q in line_first:
+        start(me, q, "across", None, True)
+
+    def along(step, q, other, cross):
+        half = 1 - side if other else side
+        lower = jnp.maximum(at - step, 0) * 2 + half
+        upper = jnp.minimum(at + step, last) * 2 + half
+        arrive(lower, q, at >= step)
+        if step < last:
+            start(lower, q, "up", (at >= step) & (at < last))
+        if cross:
+            start(lower, q, "across", at >= step)
+        arrive(upper, q, at <= last - step)
+        if step < last:
+            start(upper, q, "down", (at <= last - step) & (at > 0))
+        if cross:
+            start(upper, q, "across", at <= last - step)
+
+    for step in range(1, line):
+        if step == 1:
+            for q in pair_first:
+                arrive(across, q, None)
+                start(across, q, "up", at < last)
+                start(across, q, "down", at > 0)
+        for q in line_first:
+            along(step, q, 0, True)
+        for q in pair_first:
+            along(step, q, 0, False)
+        for q in pair_first:
+            along(step, q, 1, False)
+    for q in line_first:
+        for place in range(line):
+            arrive(place * 2 + 1 - side, q, None)
     own.wait()
-    for sent in sends:
-        sent.wait_send()
+    for condition, copy in sends:
+        if condition is None:
+            copy.wait_send()
+        else:
+            pl.when(condition)(copy.wait_send)
 
 
 def spread(rows, collective_id):
     tp_count = lax.axis_size("tp")
     count, columns = rows.shape
-    ring = tp_count // 2
-    if ring != 4 or count % 64:
+    line = tp_count // 2
+    if line != 4 or count % 128:
         return lax.all_gather(rows, "tp", axis=0, tiled=True)
     out = pl.pallas_call(
-        functools.partial(spread_kernel, ring),
+        functools.partial(spread_kernel, line),
         out_shape=jax.ShapeDtypeStruct((tp_count, count, columns), rows.dtype),
         in_specs=[VMEM_SPEC],
         out_specs=VMEM_SPEC,
         scratch_shapes=[
             pltpu.SemaphoreType.DMA,
-            pltpu.SemaphoreType.DMA((28,)),
-            pltpu.SemaphoreType.DMA((tp_count, 4)),
+            pltpu.SemaphoreType.DMA((80,)),
+            pltpu.SemaphoreType.DMA((tp_count, 5)),
         ],
         compiler_params=pltpu.CompilerParams(
             collective_id=collective_id, has_side_effects=True, vmem_limit_bytes=VMEM_LIMIT
         ),
     )(rows)
     return out.reshape(tp_count * count, columns)
+
+
+def project_kernel(slot_ref, rows_ref, gain_ref, wq_ref, wp_ref, q_ref, p_ref, sq_ref, choose, squares):
+    step = pl.program_id(1)
+    total, slots = choose.shape
+    sub = min(total, 512)
+
+    @pl.when(step == 0)
+    def _():
+        q_ref[...] = jnp.zeros_like(q_ref)
+        p_ref[...] = jnp.zeros_like(p_ref)
+        squares[...] = jnp.zeros_like(squares)
+
+        @pl.loop(0, total // 128)
+        def _(r):
+            rows = pl.ds(pl.multiple_of(r * 128, 128), 128)
+            place = lax.broadcasted_iota(jnp.int32, (128, slots), 1)
+            choose[rows] = (place == slot_ref[rows, :1]).astype(jnp.float32).astype(choose.dtype)
+
+    @pl.loop(0, total // sub)
+    def _(r):
+        rows = pl.ds(pl.multiple_of(r * sub, sub), sub)
+        embed = jnp.dot(choose[rows], rows_ref[...], preferred_element_type=jnp.float32)
+        square = embed * embed
+        folded = square[:, :128]
+        for lane in range(128, square.shape[1], 128):
+            folded = folded + square[:, lane : lane + 128]
+        squares[rows] = squares[rows] + folded
+        scaled = (embed * gain_ref[...]).astype(jnp.bfloat16)
+        q_ref[rows] = q_ref[rows] + jnp.dot(scaled, wq_ref[...], preferred_element_type=jnp.float32)
+        p_ref[rows] = p_ref[rows] + jnp.dot(scaled, wp_ref[...], preferred_element_type=jnp.float32)
+
+    @pl.when(step == pl.num_programs(1) - 1)
+    def _():
+        per = sq_ref.shape[2]
+        for block in range(sq_ref.shape[0]):
+            flipped = jnp.transpose(squares[block * per : (block + 1) * per])
+            row = jnp.sum(flipped, axis=0, keepdims=True)
+            sq_ref[block] = jnp.broadcast_to(row, (8, per))
+
+
+def project(slot, gathered, gain_here, w_query, w_pair, ctx_count):
+    tokens_all = slot.shape[0]
+    slots, columns = gathered.shape
+    tok_here = tokens_all // ctx_count
+    rows = min(tokens_all, 1024)
+    tile = min(columns, 512)
+    q_wide, p_wide = w_query.shape[1], w_pair.shape[1]
+    return pl.pallas_call(
+        project_kernel,
+        grid=(tokens_all // rows, columns // tile),
+        out_shape=[
+            jax.ShapeDtypeStruct((tokens_all, q_wide), jnp.float32),
+            jax.ShapeDtypeStruct((tokens_all, p_wide), jnp.float32),
+            jax.ShapeDtypeStruct((ctx_count, 8, tok_here), jnp.float32),
+        ],
+        in_specs=[
+            pl.BlockSpec((rows, 128), lambda i, j: (i, 0)),
+            pl.BlockSpec((slots, tile), lambda i, j: (0, j)),
+            pl.BlockSpec((1, tile), lambda i, j: (0, j)),
+            pl.BlockSpec((tile, q_wide), lambda i, j: (j, 0)),
+            pl.BlockSpec((tile, p_wide), lambda i, j: (j, 0)),
+        ],
+        out_specs=[
+            pl.BlockSpec((rows, q_wide), lambda i, j: (i, 0)),
+            pl.BlockSpec((rows, p_wide), lambda i, j: (i, 0)),
+            pl.BlockSpec((rows // tok_here, 8, tok_here), lambda i, j: (i, 0, 0)),
+        ],
+        scratch_shapes=[
+            pltpu.VMEM((rows, slots), jnp.bfloat16),
+            pltpu.VMEM((rows, 128), jnp.float32),
+        ],
+        compiler_params=pltpu.CompilerParams(
+            dimension_semantics=("arbitrary", "arbitrary"), vmem_limit_bytes=VMEM_LIMIT
+        ),
+    )(
+        jnp.broadcast_to(slot[:, None], (tokens_all, 128)),
+        gathered,
+        gain_here.reshape(1, columns),
+        w_query,
+        w_pair,
+    )
 
 
 def fold_kernel(n, pieces, arrays, *refs):
@@ -371,6 +461,12 @@
     mine = leads & (shard == tp_at)
     row_shard, row_rank = redeal(shard), redeal(rank)
 
+    kv_head = tp_at * heads_here // (HEADS // KV_HEADS)
+    w_pair = lax.dynamic_slice_in_dim(w_keyval, kv_head * HD, HD, 2).reshape(
+        w_keyval.shape[0], 2 * HD
+    )
+    gain_here = lax.dynamic_slice_in_dim(gain, ctx_at * columns, columns)
+
     def one_round(number, collective_id):
         wanted = number * capacity + jnp.arange(capacity, dtype=jnp.int32)
         hit = mine[None, :] & (rank[None, :] == wanted[:, None])
@@ -378,27 +474,16 @@
         gathered = spread(pick_rows(table, asked), collective_id)
         in_round = (row_rank >= number * capacity) & (row_rank < (number + 1) * capacity)
         slot = jnp.where(in_round, row_shard * capacity + row_rank - number * capacity, -1)
-        choose = slot[:, None] == jnp.arange(tp_count * capacity, dtype=jnp.int32)[None, :]
-        return jnp.dot(
-            choose.astype(table.dtype), gathered, preferred_element_type=jnp.float32
-        ).astype(table.dtype)
-
-    embed = one_round(0, 0)
-    embed = lax.fori_loop(1, rounds, lambda i, held: held + one_round(i, 1), embed)
-    col_embed = embed.astype(jnp.float32)
-    kv_head = tp_at * heads_here // (HEADS // KV_HEADS)
-    w_pair = lax.dynamic_slice_in_dim(w_keyval, kv_head * HD, HD, 2).reshape(
-        w_keyval.shape[0], 2 * HD
+        return tuple(project(slot, gathered, gain_here, w_query, w_pair, ctx_count))
+
+    terms = tuple(one_round(0, 0))
+    query_term, pair_term, square_term = lax.fori_loop(
+        1, rounds, lambda i, held: jax.tree.map(jnp.add, held, one_round(i, 1)), terms
     )
-    gain_here = lax.dynamic_slice_in_dim(gain, ctx_at * columns, columns)
-    col_scaled = (col_embed * gain_here).astype(jnp.bfloat16)
-    query_term = jnp.dot(col_scaled, w_query, preferred_element_type=jnp.float32)
-    pair_term = jnp.dot(col_scaled, w_pair, preferred_element_type=jnp.float32)
-    square_term = jnp.sum(col_embed * col_embed, axis=1)
     pair_raw, query_raw, sumsq = fold(
         pair_term.reshape(ctx_count, tok_here, 2 * HD),
         query_term.reshape(ctx_count, tok_here, heads_here * HD),
-        jnp.broadcast_to(square_term.reshape(ctx_count, 1, tok_here), (ctx_count, 8, tok_here)),
+        square_term,
     )
     inverse = lax.rsqrt(sumsq[0] / width + 1e-05)
     my_pos = lax.dynamic_slice_in_dim(positions, ctx_at * tok_here, tok_here)

time: 163 us -> 154 us (0.945)
  matrix products: 24 us -> 5 us
  Pallas kernels: 113 us -> 126 us
  other arithmetic: 19.1 us -> 15.3 us
    dot_general x3 -> x0, matrix products: 19 us -> none  [the longest x1 8.42 us: one_round(): jnp.dot(choose.astype(table.dtype), gathered, preferred_element_type=jnp....]
    pallas_call x1 -> x2, Pallas kernels: 57 us -> 71.5 us  [the longest x1 54.1 us: spread(): pl.pallas_call(functools.partial(spread_kernel, line), out_shape=jax.Shap...]
    reduce_sum x1 -> x0, other arithmetic: 3.65 us -> none  [shards(): square_term = jnp.sum(col_embed * col_embed, axis=1)]
where the time goes in v2:
time: 154 us; the launch traced here: 153 us
  Pallas kernels  126 us (82%)
  other arithmetic  15.3 us (10%)
  local copies, waits for them, and re-layouts  5.84 us (4%)
  matrix products  5 us (3%)
    pallas_call x1, Pallas kernels, spread(): pl.pallas_call(functools.partial(spread_kernel, line), out_shape=jax.Shap...  54.1 us
    pallas_call x1, Pallas kernels, fold(): pl.pallas_call(functools.partial(fold_kernel, n, tuple(pieces), len(array...  37.4 us
    pallas_call x1, Pallas kernels, project(): pl.pallas_call(project_kernel, grid=(tokens_all // rows, columns // tile)...  17.4 us
    pallas_call x1, Pallas kernels, share(): pl.pallas_call(functools.partial(share_kernel, n), out_shape=jax.ShapeDty...  10.4 us
    pallas_call x1, Pallas kernels, pick_rows(): pl.pallas_call(pick_kernel, out_shape=jax.ShapeDtypeStruct((count, column...  6.52 us
    reduce_sum x1, other arithmetic, shards(): totals = jnp.sum(weights, axis=1)  3.6 us

profile of v2, /device:TPU:1, one launch (start us, length us, event | category | flops | bytes accessed | tf_op | source)
XLA Modules:
  0.0 153.1 jit_solution(11496484500410042065)
XLA Ops:
  0.0 1.8 %constant_dynamic-slice_fusion = bf16[2048,2,128]{2,1,0:T(2,128)(2,1)S(1)} fusion(bf16[2048,2,1024]{2,1,0:T(2,128)(2,1)} %param.15, s32[]{:T(128)S(6)} %select_n.117), kind=kLoop, calls=%fused_computation.65 | loop fusion | bytes 2097156 | tf_op jit(solution)/shard_map/dynamic_slice | solution.py:465
  1.8 0.1 copy.28
  2.0 1.5 %select_reduce_fusion.1 = s32[1024]{0:T(1024)S(1)} fusion(s32[1024]{0:T(1024)} %param.9), kind=kLoop, calls=%fused_computation.15 | loop fusion | flops 3144704 | bytes 8192 | tf_op jit(solution)/shard_map/reduce_min | solution.py:428
  3.5 0.7 compare_and_fusion.1
  4.2 1.5 convert_reduce_fusion
  5.7 0.7 broadcast_subtract_fusion
  6.4 0.2 select_reduce_fusion.2
  6.6 0.6 and_select_fusion.2
  7.1 0.7 broadcast_in_dim.159.lane_ref
  7.8 0.0 copy-start.3
  7.8 6.5 %shard_map.73.x_ref = bf16[128,2048]{1,0:T(8,128)(2,1)} custom-call(s32[128]{0:T(128)} %get-tuple-element.249.group_ref, bf16[16032,2048]{1,0:T(8,128)(2,1)} %table_ref.1, s32[128,128]{1,0:T(8,128)} %broadcast_in_dim.159.lane_ref), custom_call_target="tpu_custom_call" | custom-call | tf_op jit(solution)/shard_map/pallas_call | solution.py:58
  14.4 54.1 %shard_map.74 = bf16[8,128,2048]{2,1,0:T(8,128)(2,1)} custom-call(bf16[128,2048]{1,0:T(8,128)(2,1)} %shard_map.73.x_ref), custom_call_target="tpu_custom_call" | custom-call | tf_op jit(solution)/shard_map/pallas_call | solution.py:180
  68.4 0.0 copy-done.3
  68.4 0.1 iota_compare_fusion.3
  68.5 0.1 select_reduce_fusion.4
  68.6 1.0 broadcast_in_dim.156.slot_ref
  69.6 0.7 dynamic_slice.10
  70.3 17.4 %shard_map.75 = (f32[1024,1024]{1,0:T(8,128)}, f32[1024,256]{1,0:T(8,128)S(1)}, f32[4,8,256]{2,1,0:T(8,128)S(1)}) custom-call(s32[1024,128]{1,0:T(8,128)} %broadcast_in_dim.156.slot_ref, bf16[1024,2048]{1,0:T(8,128)(2,1)} %bitcast.51, f32[1,2048]{1,0:T(1,128)S(1)} %bitcast.58, bf16[2048,1024]{1,0:T(8,128)(2,1)} %wq_ref.1, bf16[2048,256]{1,0:T(8,128)(2,1)S(1)} %bitcast.48), custom_call_target="tpu_custom_call" | custom-call | tf_op jit(solution)/shard_map/pallas_call | solution.py:243
  87.8 0.6 reduce_max.18
  89.1 0.2 while.16
  89.3 37.4 %shard_map.76 = (f32[256,256]{1,0:T(8,128)}, f32[256,1024]{1,0:T(8,128)}, f32[8,256]{1,0:T(8,128)}) custom-call(f32[4,256,256]{2,1,0:T(8,128)S(1)} %bitcast.50, f32[4,256,1024]{2,1,0:T(8,128)} %bitcast.47, f32[4,8,256]{2,1,0:T(8,128)S(1)} %get-tuple-element.197.refs_2_), custom_call_target="tpu_custom_call" | custom-call | tf_op jit(solution)/shard_map/pallas_call | solution.py:350
  126.7 0.0 copy-start.4
  126.7 0.7 add_rsqrt_fusion
  127.4 1.1 slice_multiply_fusion
  128.5 0.1 add_bitcast_fusion
  128.6 0.1 fusion.21
  128.7 0.6 subtract_convert_fusion.1
  129.3 0.8 pad_maximum_fusion.1.x_ref
  130.0 10.4 %shard_map.77 = bf16[4,256,256]{2,1,0:T(8,128)(2,1)} custom-call(bf16[256,256]{1,0:T(8,128)(2,1)} %pad_maximum_fusion.1.x_ref), custom_call_target="tpu_custom_call" | custom-call | tf_op jit(solution)/shard_map/pallas_call | solution.py:389
  140.4 0.0 copy-start.2
  140.4 1.4 multiply_bitcast_fusion
  141.9 0.2 copy.21
  142.1 0.3 fusion.22
  142.4 0.4 subtract_convert_fusion
  142.8 0.3 pad_maximum_fusion
  143.1 0.0 copy-done.4
  143.1 0.2 reduce-window.8
  143.3 0.1 convert_reduce_fusion.2
  143.4 0.1 convert_reduce_fusion.1
  143.5 0.0 copy-done.2
  143.5 2.1 %fusion = (f32[2048]{0:T(1024)S(1)}, f32[2048,1024]{0,1:T(8,128)S(1)}) fusion(s32[2048]{0:T(1024)S(1)} %bitcast.66, s32[2048]{0:T(1024)S(1)} %bitcast.63, s32[1024]{0:T(1024)S(1)} %add_bitcast_fusion, s32[1024]{0:T(1024)S(1)} %convert_reduce_fusion.1, bf16[2048,128]{1,0:T(8,128)(2,1)S(1)} %bitcast.54, bf16[1024,256]{1,0:T(8,128)(2,1)S(1)} %bitcast.55), kind=kOutput, calls=%fused_computation.11 | convolution fusion | flops 549451776 | bytes 9207808 | tf_op jit(solution)/shard_map/dot_general | solution.py:505
  145.6 3.6 %fusion.1 = f32[2048]{0:T(1024)S(1)} fusion(f32[2048,1024]{0,1:T(8,128)S(1)} %get-tuple-element.251, f32[2048]{0:T(1024)S(1)} %get-tuple-element.250, s32[2048]{0:T(1024)S(1)} %bitcast.67, s32[2048]{0:T(1024)S(1)} %bitcast.64, s32[1024]{0:T(1024)S(1)} %add_bitcast_fusion, s32[1024]{0:T(1024)S(1)} %convert_reduce_fusion.1), kind=kLoop, calls=%fused_computation.12 | loop fusion | flops 16775168 | bytes 8429568 | tf_op jit(solution)/shard_map/reduce_sum | solution.py:513
  149.2 2.9 %fusion.10 = bf16[2048,128]{1,0:T(8,128)(2,1)S(1)} fusion(f32[2048,1024]{0,1:T(8,128)S(1)} %get-tuple-element.251, f32[2048]{0:T(1024)S(1)} %get-tuple-element.250, s32[2048]{0:T(1024)S(1)} %bitcast.68, s32[2048]{0:T(1024)S(1)} %bitcast.65, s32[1024]{0:T(1024)S(1)} %add_bitcast_fusion, s32[1024]{0:T(1024)S(1)} %convert_reduce_fusion.1, ...), kind=kOutput, calls=%fused_computation.21 | convolution fusion | flops 554172416 | bytes 9216000 | tf_op jit(solution)/shard_map/dot_general | solution.py:514
  152.1 0.9 copy.29
  (7 shorter events, 0.0 us)
Async XLA Ops:
  7.8 60.6 %copy-start.3 = (s32[8]{0:T(128)S(1)}, s32[8]{0:T(128)}, u32[]{:S(2)}) copy-start(s32[8]{0:T(128)} %param.11) | copy-start | bytes 100
  126.7 16.4 %copy-start.4 = (s32[8]{0:T(128)S(1)}, s32[8]{0:T(128)}, u32[]{:S(2)}) copy-start(s32[8]{0:T(128)} %param.10) | copy-start | bytes 100
  140.4 3.1 %copy-start.2 = (bf16[4,256,256]{2,1,0:T(8,128)(2,1)S(1)}, bf16[4,256,256]{2,1,0:T(8,128)(2,1)}, u32[]{:S(2)}) copy-start(bf16[4,256,256]{2,1,0:T(8,128)(2,1)} %shard_map.77) | copy-start | bytes 1572868
